TPU v7x, 128 devices: a whole 4x4x4 slice. The times are simulated.
128 devices in a mesh: row: 8 (over x, core), col: 16 (over z, y).
Axes of the slice: x: 4, y: 4, z: 4, core: 2. Of those that a mesh axis runs over, the one named last changes fastest.
Arguments:
- surface_head: float32 [512, 4096], P('row', 'col'), may hold values from -6 to 6
- conduct_x: float32 [512, 4096], P('row', 'col'), may hold values from 0.01 to 0.1
- conduct_y: float32 [512, 4096], P('row', 'col'), may hold values from 0.01 to 0.1
- porosity: float32 [512, 4096], P('row', 'col'), may hold values from 0.45 to 1
- rainfall: float32 [512, 4096], P('row', 'col'), may hold values from 0.005 to 0.1
- pipe_head: float32 [32, 32768], P(None, ('row', 'col')), may hold values from -6 to 6
- pipe_class: int32 [32768], P(('row', 'col')), may hold values from 0 to 3
- pipe_up: int32 [32768], P(('row', 'col')), may hold values from 0 to 4095
- pipe_down: int32 [32768], P(('row', 'col')), may hold values from 0 to 4095
- pipe_matrices: float32 [4, 32, 32], replicated
- link_cell: int32 [128, 128, 64], P(('row', 'col')), may hold values from -1 to 16383, as said below
- link_node: int32 [128, 128, 64], P(None, ('row', 'col')), may hold values from -1 to 8191, as said below
- link_coef: float32 [128, 128, 64], P(None, ('row', 'col')), may hold values from 0.05 to 0.4
Outputs:
- surface_out: float32 [512, 4096], P('row', 'col')
- pipe_out: float32 [32, 32768], P(None, ('row', 'col'))
Inputs may be any that keep to these rules, and one draw needn't show every extreme that they name: `link_cell`: for each source tile and pipe owner the live slots come first; each is a cell of the source tile counted row by row; the other slots are -1. In every draw some tile sends 64 live slots to some owner. `link_node`: -1 exactly where link_cell is -1 at the same source tile, owner and slot; else a node of the owner's pipes, numbered node * 256 + pipe.
All inputs are finite; a program needn't handle non-finite values.
Results may differ from a plain program's by a relative error of at most 0.00015.
Values sent between devices are 32-bit elements; how exact they have to be, the bound alone decides.
No kernel may reach another device: no remote copies, remote signals or barrier semaphores. Data moves between devices by JAX's collectives and lax.ppermute only.
A program may use at most 64 MiB of HBM per device.

v0:
```python
import jax
import jax.numpy as jnp
from jax import lax
from jax.sharding import PartitionSpec as P

CLASSES = 4
SWEEPS = 4
STEPS = 3
boundary_gain = 0.5


def passed_along(block, axis, distance):
    devices = range(lax.axis_size(axis))
    route = [(i - distance, i) for i in devices if i - distance in devices]
    return lax.ppermute(block, axis, route)


def with_halo(block, sides, width):
    for axis, dim in sides:
        count = lax.axis_size(axis)
        forward = [(i, i + 1) for i in range(count - 1)]
        backward = [(target, source) for source, target in forward]
        low = lax.ppermute(
            lax.slice_in_dim(block, block.shape[dim] - width, None, axis=dim), axis, forward
        )
        high = lax.ppermute(lax.slice_in_dim(block, 0, width, axis=dim), axis, backward)
        block = jnp.concatenate([low, block, high], axis=dim)
    return block


def sweep_once(
    center, north, south, west, east, north_gain, south_gain, west_gain, east_gain, inverse, source
):
    change = (
        north_gain * (north - center)
        + south_gain * (south - center)
        + west_gain * (west - center)
        + east_gain * (east - center)
    )
    return center + change * inverse + source


def body(
    surface_head,
    conduct_x,
    conduct_y,
    porosity,
    rainfall,
    pipe_head,
    pipe_class,
    pipe_up,
    pipe_down,
    pipe_matrices,
    link_cell,
    link_node,
    link_coef,
):
    tile_rows, tile_cols = surface_head.shape
    inverse = 1.0 / porosity
    from_above = passed_along(conduct_x[-1:, :], "row", 1)
    north_gain = jnp.concatenate([from_above, conduct_x[:-1, :]], axis=0)
    from_left = passed_along(conduct_y[:, -1:], "col", 1)
    west_gain = jnp.concatenate([from_left, conduct_y[:, :-1]], axis=1)
    cell_index = link_cell[0]
    cell_live = cell_index >= 0
    cell_safe = jnp.where(cell_live, cell_index, 0)
    node_index = link_node[:, 0, :]
    node_live = node_index >= 0
    node_safe = jnp.where(node_live, node_index, 0)
    link_gain = link_coef[:, 0, :]
    inverse_flat = inverse.reshape(-1)
    surface = surface_head
    pipe_state = pipe_head
    for coupling_step in range(STEPS):
        for sweep_index in range(SWEEPS):
            padded = with_halo(surface, (("row", 0), ("col", 1)), 1)
            surface = sweep_once(
                surface,
                padded[:-2, 1:-1],
                padded[2:, 1:-1],
                padded[1:-1, :-2],
                padded[1:-1, 2:],
                north_gain,
                conduct_x,
                west_gain,
                conduct_y,
                inverse,
                rainfall,
            )
        surface_flat = surface.reshape(-1)
        sent_heads = jnp.where(cell_live, surface_flat[cell_safe], 0.0)
        pipe_flat = pipe_state.reshape(-1)
        pipe_at_slots = jnp.where(node_live, pipe_flat[node_safe], 0.0)
        arrived = lax.all_to_all(
            sent_heads, ("row", "col"), split_axis=0, concat_axis=0, tiled=True
        )
        manhole_flow = jnp.where(node_live, link_gain * (arrived - pipe_at_slots), 0.0)
        inflow = jnp.zeros_like(pipe_flat).at[node_safe].add(manhole_flow).reshape(pipe_state.shape)
        returned = lax.all_to_all(
            manhole_flow, ("row", "col"), split_axis=0, concat_axis=0, tiled=True
        )
        surface = (
            surface_flat.at[cell_safe]
            .add(-(returned * inverse_flat[cell_safe]))
            .reshape(tile_rows, tile_cols)
        )
        first_heads, last_heads = (
            lax.all_gather(pipe_state[0], "col", axis=0, tiled=True),
            lax.all_gather(pipe_state[-1], "col", axis=0, tiled=True),
        )
        balance = pipe_state + inflow
        balance = balance.at[0].add(boundary_gain * last_heads[pipe_up])
        balance = balance.at[-1].add(boundary_gain * first_heads[pipe_down])
        updated = jnp.zeros_like(pipe_state)
        for class_index in range(CLASSES):
            product = jnp.dot(
                pipe_matrices[class_index],
                balance,
                precision=lax.Precision.HIGHEST,
                preferred_element_type=jnp.float32,
            )
            updated = jnp.where(pipe_class[None, :] == class_index, product, updated)
        pipe_state = updated
    return (surface, pipe_state)


def solution(mesh):
    placed = (
        P("row", "col"),
        P("row", "col"),
        P("row", "col"),
        P("row", "col"),
        P("row", "col"),
        P(None, ("row", "col")),
        P(("row", "col")),
        P(("row", "col")),
        P(("row", "col")),
        P(),
        P(("row", "col"), None, None),
        P(None, ("row", "col"), None),
        P(None, ("row", "col"), None),
    )
    return jax.shard_map(
        body,
        mesh=mesh,
        in_specs=placed,
        out_specs=(P("row", "col"), P(None, ("row", "col"))),
        check_vma=False,
    )
```

profile of v0, /device:TPU:1, one launch (start us, length us, event | category | flops | bytes accessed | tf_op | source)
XLA Modules:
  0.0 1038.9 jit_solution(1538303368657251957)
XLA Ops:
  38.3 23.2 %all-gather = f32[1,4096]{1,0:T(1,128)S(1)} all-gather(f32[1,256]{1,0:T(1,128)S(1)} %get-tuple-element.133), channel_id=2, replica_groups=mesh['row'=8,'col'=16] {'col'}, dimensions={1}, use_global_device_ids=true | all-gather | bytes 17408 | tf_op jit(solution)/shard_map/all_gather | solution.py:109
  63.3 7.5 collective-permute-start.11
  84.8 5.3 collective-permute-start.14
  96.8 19.4 %all-gather.1 = f32[1,4096]{1,0:T(1,128)S(1)} all-gather(f32[1,256]{1,0:T(1,128)S(1)} %get-tuple-element.132), channel_id=3, replica_groups=mesh['row'=8,'col'=16] {'col'}, dimensions={1}, use_global_device_ids=true | all-gather | bytes 17408 | tf_op jit(solution)/shard_map/all_gather | solution.py:108
  118.2 45.5 %gather_fusion = f32[8192]{0:T(1024)S(1)} fusion(f32[16384]{0:T(1024)S(1)} %bitcast.123, s32[8192]{0:T(1024)S(1)} %broadcast_clamp_fusion.1), kind=kCustom, calls=%fused_computation | custom fusion | bytes 98304 | tf_op jit(solution)/shard_map/gather | solution.py:91
  164.5 12.9 %all-to-all-start = ((f32[128,1,64]{2,1,0:T(1,128)}), f32[128,1,64]{2,1,0:T(1,128)S(1)}, u32[]{:S(2)}, u32[]{:S(2)}) async-start(f32[128,1,64]{2,1,0:T(1,128)} %bitcast.2), calls=%async_computation | async-start | bytes 131072 | tf_op jit(solution)/shard_map/all_to_all | solution.py:94
  177.5 45.5 %gather_fusion.1 = f32[8192]{0:T(1024)S(1)} fusion(f32[8192]{0:T(1024)S(1)} %bitcast.130, s32[8192]{0:T(1024)S(1)} %broadcast_clamp_fusion), kind=kCustom, calls=%fused_computation.1 | custom fusion | bytes 98304 | tf_op jit(solution)/shard_map/gather | solution.py:93
  224.1 45.5 %gather_fusion.2 = f32[8192]{0:T(1024)S(1)} fusion(f32[16384]{0:T(1024)S(1)} %bitcast.132, s32[8192]{0:T(1024)S(1)} %broadcast_clamp_fusion.1), kind=kCustom, calls=%fused_computation.2 | custom fusion | bytes 98304 | tf_op jit(solution)/shard_map/gather | solution.py:104
  270.3 9.8 all-to-all-start.1
  280.2 44.9 %scatter_custom_fusion.1 = f32[8192]{0:T(1024)S(1)} fusion(s32[8192]{0:T(1024)S(1)} %reshape.369, f32[8192]{0:T(1024)S(1)} %reshape.475, f32[]{:T(128)} %constant.152.clone.1), kind=kCustom, calls=%fused_computation.362 | custom fusion | flops 8192 | bytes 32772 | tf_op jit(solution)/shard_map/scatter-add | solution.py:98
  325.3 50.3 %scatter_fusion = f32[16384]{0:T(1024)S(1)} fusion(f32[16384]{0:T(1024)S(1)} %bitcast.124, s32[8192]{0:T(1024)S(1)} %reshape.465, f32[8192]{0:T(1024)S(1)} %reshape.467), kind=kCustom, calls=%fused_computation.13 | custom fusion | flops 8192 | bytes 131072 | tf_op jit(solution)/shard_map/scatter-add | solution.py:104
  383.4 9.8 collective-permute-start.20
  422.8 25.7 %all-gather.2 = f32[1,4096]{1,0:T(1,128)S(1)} all-gather(f32[1,256]{1,0:T(1,128)S(1)} %get-tuple-element.131), channel_id=4, replica_groups=mesh['row'=8,'col'=16] {'col'}, dimensions={1}, use_global_device_ids=true | all-gather | bytes 17408 | tf_op jit(solution)/shard_map/all_gather | solution.py:109
  455.6 7.0 collective-permute-start.30
  468.7 17.2 %all-gather.3 = f32[1,4096]{1,0:T(1,128)S(1)} all-gather(f32[1,256]{1,0:T(1,128)S(1)} %get-tuple-element.130), channel_id=5, replica_groups=mesh['row'=8,'col'=16] {'col'}, dimensions={1}, use_global_device_ids=true | all-gather | bytes 17408 | tf_op jit(solution)/shard_map/all_gather | solution.py:108
  487.8 45.5 %gather_fusion.3 = f32[8192]{0:T(1024)S(1)} fusion(f32[16384]{0:T(1024)S(1)} %bitcast.125, s32[8192]{0:T(1024)S(1)} %broadcast_clamp_fusion.1), kind=kCustom, calls=%fused_computation.3 | custom fusion | bytes 98304 | tf_op jit(solution)/shard_map/gather | solution.py:91
  534.1 13.1 %all-to-all-start.2 = ((f32[128,1,64]{2,1,0:T(1,128)}), f32[128,1,64]{2,1,0:T(1,128)S(1)}, u32[]{:S(2)}, u32[]{:S(2)}) async-start(f32[128,1,64]{2,1,0:T(1,128)} %bitcast.9), calls=%async_computation.2 | async-start | bytes 131072 | tf_op jit(solution)/shard_map/all_to_all | solution.py:94
  547.2 45.5 %gather_fusion.6 = f32[8192]{0:T(1024)S(1)} fusion(f32[8192]{0:T(1024)S(1)} %bitcast.131, s32[8192]{0:T(1024)S(1)} %broadcast_clamp_fusion), kind=kCustom, calls=%fused_computation.6 | custom fusion | bytes 98304 | tf_op jit(solution)/shard_map/gather | solution.py:93
  593.5 9.8 all-to-all-start.3
  603.4 44.9 %scatter_custom_fusion.3 = f32[8192]{0:T(1024)S(1)} fusion(s32[8192]{0:T(1024)S(1)} %reshape.369, f32[8192]{0:T(1024)S(1)} %reshape.491, f32[]{:T(128)} %constant.152.clone.1), kind=kCustom, calls=%fused_computation.360 | custom fusion | flops 8192 | bytes 32772 | tf_op jit(solution)/shard_map/scatter-add | solution.py:98
  648.6 50.3 %scatter_fusion.1 = f32[16384]{0:T(1024)S(1)} fusion(f32[16384]{0:T(1024)S(1)} %bitcast.126, s32[8192]{0:T(1024)S(1)} %reshape.465, f32[8192]{0:T(1024)S(1)} %reshape.483), kind=kCustom, calls=%fused_computation.15 | custom fusion | flops 8192 | bytes 131072 | tf_op jit(solution)/shard_map/scatter-add | solution.py:104
  706.6 9.8 collective-permute-start.36
  746.0 25.7 %all-gather.4 = f32[1,4096]{1,0:T(1,128)S(1)} all-gather(f32[1,256]{1,0:T(1,128)S(1)} %get-tuple-element.129), channel_id=6, replica_groups=mesh['row'=8,'col'=16] {'col'}, dimensions={1}, use_global_device_ids=true | all-gather | bytes 17408 | tf_op jit(solution)/shard_map/all_gather | solution.py:109
  778.8 7.0 collective-permute-start.46
  791.9 17.2 %all-gather.5 = f32[1,4096]{1,0:T(1,128)S(1)} all-gather(f32[1,256]{1,0:T(1,128)S(1)} %get-tuple-element.128), channel_id=7, replica_groups=mesh['row'=8,'col'=16] {'col'}, dimensions={1}, use_global_device_ids=true | all-gather | bytes 17408 | tf_op jit(solution)/shard_map/all_gather | solution.py:108
  811.0 45.5 %gather_fusion.7 = f32[8192]{0:T(1024)S(1)} fusion(f32[16384]{0:T(1024)S(1)} %bitcast.127, s32[8192]{0:T(1024)S(1)} %broadcast_clamp_fusion.1), kind=kCustom, calls=%fused_computation.7 | custom fusion | bytes 98304 | tf_op jit(solution)/shard_map/gather | solution.py:91
  857.3 13.1 %all-to-all-start.4 = ((f32[128,1,64]{2,1,0:T(1,128)}), f32[128,1,64]{2,1,0:T(1,128)S(1)}, u32[]{:S(2)}, u32[]{:S(2)}) async-start(f32[128,1,64]{2,1,0:T(1,128)} %bitcast.27), calls=%async_computation.4 | async-start | bytes 131072 | tf_op jit(solution)/shard_map/all_to_all | solution.py:94
  870.4 45.5 %gather_fusion.10 = f32[8192]{0:T(1024)S(1)} fusion(f32[8192]{0:T(1024)S(1)} %bitcast.129, s32[8192]{0:T(1024)S(1)} %broadcast_clamp_fusion), kind=kCustom, calls=%fused_computation.10 | custom fusion | bytes 98304 | tf_op jit(solution)/shard_map/gather | solution.py:93
  916.2 44.9 %scatter_custom_fusion.5 = f32[8192]{0:T(1024)S(1)} fusion(s32[8192]{0:T(1024)S(1)} %reshape.369, f32[8192]{0:T(1024)S(1)} %reshape.507, f32[]{:T(128)} %constant.152.clone.1), kind=kCustom, calls=%fused_computation.358 | custom fusion | flops 8192 | bytes 32772 | tf_op jit(solution)/shard_map/scatter-add | solution.py:98
  962.4 15.8 %all-to-all-start.5 = ((f32[128,1,64]{2,1,0:T(1,128)}), f32[128,1,64]{2,1,0:T(1,128)S(1)}, u32[]{:S(2)}, u32[]{:S(2)}) async-start(f32[128,1,64]{2,1,0:T(1,128)} %bitcast.35), calls=%async_computation.5 | async-start | bytes 131072 | tf_op jit(solution)/shard_map/all_to_all | solution.py:99
  979.0 8.9 all-to-all-done.5
  988.0 50.3 %scatter_fusion.2 = f32[16384]{0:T(1024)S(1)} fusion(f32[16384]{0:T(1024)S(1)} %bitcast.128, s32[8192]{0:T(1024)S(1)} %reshape.465, f32[8192]{0:T(1024)S(1)} %reshape.499), kind=kCustom, calls=%fused_computation.17 | custom fusion | flops 8192 | bytes 131072 | tf_op jit(solution)/shard_map/scatter-add | solution.py:104
  (275 shorter events, 174.2 us)
Async XLA Ops:
  1.4 17.1 %collective-permute-start.2 = (f32[1,256]{1,0:T(1,128)S(1)}, f32[1,256]{1,0:T(1,128)S(1)}, u32[]{:S(2)}, u32[]{:S(2)}) collective-permute-start(f32[1,256]{1,0:T(1,128)S(1)} %get-tuple-element.127), channel_id=1, source_target_pairs={{16,0},{32,16},{48,32},{64,48},{80,64},{96,80},{112,96},{17,1},{33... | collective-permute-start | bytes 3080 | tf_op jit(solution)/shard_map/ppermute | solution.py:26
  4.7 13.8 %collective-permute-start.1 = (f32[1,256]{1,0:T(1,128)S(1)}, f32[1,256]{1,0:T(1,128)S(1)}, u32[]{:S(2)}, u32[]{:S(2)}) collective-permute-start(f32[1,256]{1,0:T(1,128)S(1)} %get-tuple-element.126), channel_id=1, source_target_pairs={{0,16},{16,32},{32,48},{48,64},{64,80},{80,96},{96,112},{1,17},{17... | collective-permute-start | bytes 3080 | tf_op jit(solution)/shard_map/ppermute | solution.py:23
  8.5 15.5 %collective-permute-start = (f32[1,256]{1,0:T(1,128)S(1)}, f32[1,256]{1,0:T(1,128)S(1)}, u32[]{:S(2)}, u32[]{:S(2)}) collective-permute-start(f32[1,256]{1,0:T(1,128)S(1)} %slice.500), channel_id=1, source_target_pairs={{0,16},{16,32},{32,48},{48,64},{64,80},{80,96},{96,112},{1,17},{17... | collective-permute-start | bytes 3080 | tf_op jit(solution)/shard_map/ppermute | solution.py:15
  11.9 12.2 %collective-permute-start.3 = (f32[64,1]{1,0:T(8,128)S(1)}, f32[64,1]{1,0:T(8,128)S(1)}, u32[]{:S(2)}, u32[]{:S(2)}) collective-permute-start(f32[64,1]{1,0:T(8,128)S(1)} %slice.506), channel_id=1, source_target_pairs={{0,1},{1,2},{2,3},{3,4},{4,5},{5,6},{6,7},{7,8},{8,9},{9,10},{10,1... | collective-permute-start | bytes 776 | tf_op jit(solution)/shard_map/ppermute | solution.py:15
  32.4 30.8 %collective-permute-start.9 = (f32[66,1]{1,0:T(8,128)S(1)}, f32[66,1]{1,0:T(8,128)S(1)}, u32[]{:S(2)}, u32[]{:S(2)}) collective-permute-start(f32[66,1]{1,0:T(8,128)S(1)} %get-tuple-element.101), channel_id=1, source_target_pairs={{1,0},{2,1},{3,2},{4,3},{5,4},{6,5},{7,6},{8,7},{9,8},{10,9},{11,1... | collective-permute-start | bytes 800 | tf_op jit(solution)/shard_map/ppermute | solution.py:26
  33.7 29.5 %collective-permute-start.8 = (f32[66,1]{1,0:T(8,128)S(1)}, f32[66,1]{1,0:T(8,128)S(1)}, u32[]{:S(2)}, u32[]{:S(2)}) collective-permute-start(f32[66,1]{1,0:T(8,128)S(1)} %get-tuple-element.100), channel_id=1, source_target_pairs={{0,1},{1,2},{2,3},{3,4},{4,5},{5,6},{6,7},{7,8},{8,9},{9,10},{10,1... | collective-permute-start | bytes 800 | tf_op jit(solution)/shard_map/ppermute | solution.py:23
  63.3 12.2 %collective-permute-start.11 = (f32[1,256]{1,0:T(1,128)S(1)}, f32[1,256]{1,0:T(1,128)S(1)}, u32[]{:S(2)}, u32[]{:S(2)}) collective-permute-start(f32[1,256]{1,0:T(1,128)S(1)} %get-tuple-element.123), channel_id=1, source_target_pairs={{16,0},{32,16},{48,32},{64,48},{80,64},{96,80},{112,96},{17,1},{33... | collective-permute-start | bytes 3080 | tf_op jit(solution)/shard_map/ppermute | solution.py:26
  82.9 7.3 collective-permute-start.15
  90.9 27.1 %collective-permute-start.17 = (f32[66,1]{1,0:T(8,128)S(1)}, f32[66,1]{1,0:T(8,128)S(1)}, u32[]{:S(2)}, u32[]{:S(2)}) collective-permute-start(f32[66,1]{1,0:T(8,128)S(1)} %get-tuple-element.97), channel_id=1, source_target_pairs={{1,0},{2,1},{3,2},{4,3},{5,4},{6,5},{7,6},{8,7},{9,8},{10,9},{11,1... | collective-permute-start | bytes 800 | tf_op jit(solution)/shard_map/ppermute | solution.py:26
  92.2 25.8 %collective-permute-start.16 = (f32[66,1]{1,0:T(8,128)S(1)}, f32[66,1]{1,0:T(8,128)S(1)}, u32[]{:S(2)}, u32[]{:S(2)}) collective-permute-start(f32[66,1]{1,0:T(8,128)S(1)} %get-tuple-element.96), channel_id=1, source_target_pairs={{0,1},{1,2},{2,3},{3,4},{4,5},{5,6},{6,7},{7,8},{8,9},{9,10},{10,1... | collective-permute-start | bytes 800 | tf_op jit(solution)/shard_map/ppermute | solution.py:23
  164.5 105.2 %all-to-all-start = ((f32[128,1,64]{2,1,0:T(1,128)}), f32[128,1,64]{2,1,0:T(1,128)S(1)}, u32[]{:S(2)}, u32[]{:S(2)}) async-start(f32[128,1,64]{2,1,0:T(1,128)} %bitcast.2), calls=%async_computation | async-start | bytes 131072 | tf_op jit(solution)/shard_map/all_to_all | solution.py:94
  270.3 54.9 %all-to-all-start.1 = ((f32[128,1,64]{2,1,0:T(1,128)}), f32[128,1,64]{2,1,0:T(1,128)S(1)}, u32[]{:S(2)}, u32[]{:S(2)}) async-start(f32[128,1,64]{2,1,0:T(1,128)} %bitcast.5), calls=%async_computation.1 | async-start | bytes 131072 | tf_op jit(solution)/shard_map/all_to_all | solution.py:99
  382.1 11.3 %collective-permute-start.21 = (f32[66,1]{1,0:T(8,128)S(1)}, f32[66,1]{1,0:T(8,128)S(1)}, u32[]{:S(2)}, u32[]{:S(2)}) collective-permute-start(f32[66,1]{1,0:T(8,128)S(1)} %get-tuple-element.95), channel_id=1, source_target_pairs={{1,0},{2,1},{3,2},{4,3},{5,4},{6,5},{7,6},{8,7},{9,8},{10,9},{11,1... | collective-permute-start | bytes 800 | tf_op jit(solution)/shard_map/ppermute | solution.py:26
  383.4 10.9 %collective-permute-start.20 = (f32[66,1]{1,0:T(8,128)S(1)}, f32[66,1]{1,0:T(8,128)S(1)}, u32[]{:S(2)}, u32[]{:S(2)}) collective-permute-start(f32[66,1]{1,0:T(8,128)S(1)} %get-tuple-element.94), channel_id=1, source_target_pairs={{0,1},{1,2},{2,3},{3,4},{4,5},{5,6},{6,7},{7,8},{8,9},{9,10},{10,1... | collective-permute-start | bytes 800 | tf_op jit(solution)/shard_map/ppermute | solution.py:23
  416.9 33.3 %collective-permute-start.29 = (f32[66,1]{1,0:T(8,128)S(1)}, f32[66,1]{1,0:T(8,128)S(1)}, u32[]{:S(2)}, u32[]{:S(2)}) collective-permute-start(f32[66,1]{1,0:T(8,128)S(1)} %get-tuple-element.91), channel_id=1, source_target_pairs={{1,0},{2,1},{3,2},{4,3},{5,4},{6,5},{7,6},{8,7},{9,8},{10,9},{11,1... | collective-permute-start | bytes 800 | tf_op jit(solution)/shard_map/ppermute | solution.py:26
  418.2 32.0 %collective-permute-start.28 = (f32[66,1]{1,0:T(8,128)S(1)}, f32[66,1]{1,0:T(8,128)S(1)}, u32[]{:S(2)}, u32[]{:S(2)}) collective-permute-start(f32[66,1]{1,0:T(8,128)S(1)} %get-tuple-element.90), channel_id=1, source_target_pairs={{0,1},{1,2},{2,3},{3,4},{4,5},{5,6},{6,7},{7,8},{8,9},{9,10},{10,1... | collective-permute-start | bytes 800 | tf_op jit(solution)/shard_map/ppermute | solution.py:23
  450.4 12.2 %collective-permute-start.31 = (f32[1,256]{1,0:T(1,128)S(1)}, f32[1,256]{1,0:T(1,128)S(1)}, u32[]{:S(2)}, u32[]{:S(2)}) collective-permute-start(f32[1,256]{1,0:T(1,128)S(1)} %get-tuple-element.113), channel_id=1, source_target_pairs={{16,0},{32,16},{48,32},{64,48},{80,64},{96,80},{112,96},{17,1},{33... | collective-permute-start | bytes 3080 | tf_op jit(solution)/shard_map/ppermute | solution.py:26
  455.6 7.7 collective-permute-start.30
  463.4 24.2 %collective-permute-start.33 = (f32[66,1]{1,0:T(8,128)S(1)}, f32[66,1]{1,0:T(8,128)S(1)}, u32[]{:S(2)}, u32[]{:S(2)}) collective-permute-start(f32[66,1]{1,0:T(8,128)S(1)} %get-tuple-element.89), channel_id=1, source_target_pairs={{1,0},{2,1},{3,2},{4,3},{5,4},{6,5},{7,6},{8,7},{9,8},{10,9},{11,1... | collective-permute-start | bytes 800 | tf_op jit(solution)/shard_map/ppermute | solution.py:26
  464.7 22.9 %collective-permute-start.32 = (f32[66,1]{1,0:T(8,128)S(1)}, f32[66,1]{1,0:T(8,128)S(1)}, u32[]{:S(2)}, u32[]{:S(2)}) collective-permute-start(f32[66,1]{1,0:T(8,128)S(1)} %get-tuple-element.88), channel_id=1, source_target_pairs={{0,1},{1,2},{2,3},{3,4},{4,5},{5,6},{6,7},{7,8},{8,9},{9,10},{10,1... | collective-permute-start | bytes 800 | tf_op jit(solution)/shard_map/ppermute | solution.py:23
  534.1 58.8 %all-to-all-start.2 = ((f32[128,1,64]{2,1,0:T(1,128)}), f32[128,1,64]{2,1,0:T(1,128)S(1)}, u32[]{:S(2)}, u32[]{:S(2)}) async-start(f32[128,1,64]{2,1,0:T(1,128)} %bitcast.9), calls=%async_computation.2 | async-start | bytes 131072 | tf_op jit(solution)/shard_map/all_to_all | solution.py:94
  593.5 54.9 %all-to-all-start.3 = ((f32[128,1,64]{2,1,0:T(1,128)}), f32[128,1,64]{2,1,0:T(1,128)S(1)}, u32[]{:S(2)}, u32[]{:S(2)}) async-start(f32[128,1,64]{2,1,0:T(1,128)} %bitcast.23), calls=%async_computation.3 | async-start | bytes 131072 | tf_op jit(solution)/shard_map/all_to_all | solution.py:99
  705.3 11.3 %collective-permute-start.37 = (f32[66,1]{1,0:T(8,128)S(1)}, f32[66,1]{1,0:T(8,128)S(1)}, u32[]{:S(2)}, u32[]{:S(2)}) collective-permute-start(f32[66,1]{1,0:T(8,128)S(1)} %get-tuple-element.87), channel_id=1, source_target_pairs={{1,0},{2,1},{3,2},{4,3},{5,4},{6,5},{7,6},{8,7},{9,8},{10,9},{11,1... | collective-permute-start | bytes 800 | tf_op jit(solution)/shard_map/ppermute | solution.py:26
  706.6 10.9 %collective-permute-start.36 = (f32[66,1]{1,0:T(8,128)S(1)}, f32[66,1]{1,0:T(8,128)S(1)}, u32[]{:S(2)}, u32[]{:S(2)}) collective-permute-start(f32[66,1]{1,0:T(8,128)S(1)} %get-tuple-element.86), channel_id=1, source_target_pairs={{0,1},{1,2},{2,3},{3,4},{4,5},{5,6},{6,7},{7,8},{8,9},{9,10},{10,1... | collective-permute-start | bytes 800 | tf_op jit(solution)/shard_map/ppermute | solution.py:23
  740.2 33.3 %collective-permute-start.45 = (f32[66,1]{1,0:T(8,128)S(1)}, f32[66,1]{1,0:T(8,128)S(1)}, u32[]{:S(2)}, u32[]{:S(2)}) collective-permute-start(f32[66,1]{1,0:T(8,128)S(1)} %get-tuple-element.83), channel_id=1, source_target_pairs={{1,0},{2,1},{3,2},{4,3},{5,4},{6,5},{7,6},{8,7},{9,8},{10,9},{11,1... | collective-permute-start | bytes 800 | tf_op jit(solution)/shard_map/ppermute | solution.py:26
  741.5 32.0 %collective-permute-start.44 = (f32[66,1]{1,0:T(8,128)S(1)}, f32[66,1]{1,0:T(8,128)S(1)}, u32[]{:S(2)}, u32[]{:S(2)}) collective-permute-start(f32[66,1]{1,0:T(8,128)S(1)} %get-tuple-element.82), channel_id=1, source_target_pairs={{0,1},{1,2},{2,3},{3,4},{4,5},{5,6},{6,7},{7,8},{8,9},{9,10},{10,1... | collective-permute-start | bytes 800 | tf_op jit(solution)/shard_map/ppermute | solution.py:23
  773.6 12.2 %collective-permute-start.47 = (f32[1,256]{1,0:T(1,128)S(1)}, f32[1,256]{1,0:T(1,128)S(1)}, u32[]{:S(2)}, u32[]{:S(2)}) collective-permute-start(f32[1,256]{1,0:T(1,128)S(1)} %get-tuple-element.105), channel_id=1, source_target_pairs={{16,0},{32,16},{48,32},{64,48},{80,64},{96,80},{112,96},{17,1},{33... | collective-permute-start | bytes 3080 | tf_op jit(solution)/shard_map/ppermute | solution.py:26
  778.8 7.7 collective-permute-start.46
  786.6 24.2 %collective-permute-start.49 = (f32[66,1]{1,0:T(8,128)S(1)}, f32[66,1]{1,0:T(8,128)S(1)}, u32[]{:S(2)}, u32[]{:S(2)}) collective-permute-start(f32[66,1]{1,0:T(8,128)S(1)} %get-tuple-element.81), channel_id=1, source_target_pairs={{1,0},{2,1},{3,2},{4,3},{5,4},{6,5},{7,6},{8,7},{9,8},{10,9},{11,1... | collective-permute-start | bytes 800 | tf_op jit(solution)/shard_map/ppermute | solution.py:26
  787.9 22.9 %collective-permute-start.48 = (f32[66,1]{1,0:T(8,128)S(1)}, f32[66,1]{1,0:T(8,128)S(1)}, u32[]{:S(2)}, u32[]{:S(2)}) collective-permute-start(f32[66,1]{1,0:T(8,128)S(1)} %get-tuple-element.80), channel_id=1, source_target_pairs={{0,1},{1,2},{2,3},{3,4},{4,5},{5,6},{6,7},{7,8},{8,9},{9,10},{10,1... | collective-permute-start | bytes 800 | tf_op jit(solution)/shard_map/ppermute | solution.py:23
  857.3 58.8 %all-to-all-start.4 = ((f32[128,1,64]{2,1,0:T(1,128)}), f32[128,1,64]{2,1,0:T(1,128)S(1)}, u32[]{:S(2)}, u32[]{:S(2)}) async-start(f32[128,1,64]{2,1,0:T(1,128)} %bitcast.27), calls=%async_computation.4 | async-start | bytes 131072 | tf_op jit(solution)/shard_map/all_to_all | solution.py:94
  962.4 25.5 %all-to-all-start.5 = ((f32[128,1,64]{2,1,0:T(1,128)}), f32[128,1,64]{2,1,0:T(1,128)S(1)}, u32[]{:S(2)}, u32[]{:S(2)}) async-start(f32[128,1,64]{2,1,0:T(1,128)} %bitcast.35), calls=%async_computation.5 | async-start | bytes 131072 | tf_op jit(solution)/shard_map/all_to_all | solution.py:99
  (37 other events, 233.2 us)
where the time goes:
time: 1040 us
  local copies, waits for them, and re-layouts  339 us (33%)
  other arithmetic  291 us (28%)
  starting transfers between devices  254 us (24%)
  blocking collectives  128 us (12%)
  waiting for transfers between devices  21.3 us (2%)
    scatter-add x3, other arithmetic, body(): surface = surface_flat.at[cell_safe].add(-(returned * inverse_flat[cell_s...  151 us
    gather x9, local copies, waits for them, and re-layouts, body(): pipe_at_slots = jnp.where(node_live, pipe_flat[node_safe], 0.0)  137 us
    gather x6, local copies, waits for them, and re-layouts, body(): sent_heads = jnp.where(cell_live, surface_flat[cell_safe], 0.0)  137 us
    scatter-add x3, other arithmetic, body(): jnp.zeros_like(pipe_flat).at[node_safe].add(manhole_flow)  135 us
    ppermute x24, starting transfers between devices, with_halo(): lax.ppermute(lax.slice_in_dim(block, block.shape[dim] - width, None, axis...  118 us
    all_gather x3, blocking collectives, body(): lax.all_gather(pipe_state[-1], 'col', axis=0, tiled=True)  74.5 us
    ppermute x24, starting transfers between devices, with_halo(): lax.ppermute(lax.slice_in_dim(block, 0, width, axis=dim), axis, backward)  56 us
    all_gather x3, blocking collectives, body(): lax.all_gather(pipe_state[0], 'col', axis=0, tiled=True)  53.8 us
  transfers between devices with their start and end apart: 56, of which 18 were waited for; matrix products, arithmetic and copies ran while one was open for 28% of the time, Pallas kernels for 0%

commit v1 on v0

--- a/solution.py
+++ b/solution.py
@@ -7,6 +7,11 @@
 SWEEPS = 4
 STEPS = 3
 boundary_gain = 0.5
+
+
+def swapped_in(array, axis, dim):
+    sent = jnp.stack([array] * lax.axis_size(axis))
+    return jnp.concatenate(lax.all_to_all(sent, axis, 0, 0), axis=dim)
 
 
 def passed_along(block, axis, distance):
@@ -105,7 +110,7 @@
             .reshape(tile_rows, tile_cols)
         )
         first_heads, last_heads = (
-            lax.all_gather(pipe_state[0], "col", axis=0, tiled=True),
+            swapped_in(pipe_state[0], "col", 0),
             lax.all_gather(pipe_state[-1], "col", axis=0, tiled=True),
         )
         balance = pipe_state + inflow

time: 1040 us -> 1010 us (0.971)
  blocking collectives: 128 us -> 74.2 us
  waiting for transfers between devices: 21.3 us -> 48.3 us
    all_gather x3 -> x0, blocking collectives: 53.8 us -> none  [body(): lax.all_gather(pipe_state[0], 'col', axis=0, tiled=True)]
    all_to_all x3, waiting for transfers between devices: 0.01 us -> 27.4 us  [body(): lax.all_to_all(sent_heads, ('row', 'col'), split_axis=0, concat_axis=0, t...]
    all_to_all x3, starting transfers between devices: 35.3 us -> 18.4 us  [body(): lax.all_to_all(manhole_flow, ('row', 'col'), split_axis=0, concat_axis=0,...]
    all_to_all x0 -> x3, starting transfers between devices: none -> 15 us  [swapped_in(): return jnp.concatenate(lax.all_to_all(sent, axis, 0, 0), axis=dim)]
  transfers between devices with their start and end apart: 56 -> 59, of which waited for: 18 -> 20; matrix products, arithmetic and copies ran while one was open for 28% -> 34% of each run, Pallas kernels for 0% -> 0%
where the time goes in v1:
time: 1010 us; the launch traced here: 1000 us
  local copies, waits for them, and re-layouts  340 us (34%)
  other arithmetic  291 us (29%)
  starting transfers between devices  244 us (24%)
  blocking collectives  74.2 us (7%)
  waiting for transfers between devices  48.3 us (5%)
    scatter-add x3, other arithmetic, body(): surface = surface_flat.at[cell_safe].add(-(returned * inverse_flat[cell_s...  151 us
    gather x9, local copies, waits for them, and re-layouts, body(): pipe_at_slots = jnp.where(node_live, pipe_flat[node_safe], 0.0)  137 us
    gather x6, local copies, waits for them, and re-layouts, body(): sent_heads = jnp.where(cell_live, surface_flat[cell_safe], 0.0)  137 us
    scatter-add x3, other arithmetic, body(): jnp.zeros_like(pipe_flat).at[node_safe].add(manhole_flow)  135 us
    ppermute x24, starting transfers between devices, with_halo(): lax.ppermute(lax.slice_in_dim(block, block.shape[dim] - width, None, axis...  118 us
    all_gather x3, blocking collectives, body(): lax.all_gather(pipe_state[-1], 'col', axis=0, tiled=True)  74.2 us
    ppermute x24, starting transfers between devices, with_halo(): lax.ppermute(lax.slice_in_dim(block, 0, width, axis=dim), axis, backward)  56.2 us
    gather x2, local copies, waits for them, and re-layouts, body(): inverse_flat[cell_safe]  45.6 us
  transfers between devices with their start and end apart: 59, of which 20 were waited for; matrix products, arithmetic and copies ran while one was open for 34% of the time, Pallas kernels for 0%

profile of v1, /device:TPU:1, one launch (start us, length us, event | category | flops | bytes accessed | tf_op | source)
XLA Modules:
  0.0 1003.0 jit_solution(121059017126330213)
XLA Ops:
  15.8 7.5 all-to-all-start.3
  46.2 22.8 %all-gather = f32[1,4096]{1,0:T(1,128)S(1)} all-gather(f32[1,256]{1,0:T(1,128)S(1)} %get-tuple-element.133), channel_id=2, replica_groups=mesh['row'=8,'col'=16] {'col'}, dimensions={1}, use_global_device_ids=true | all-gather | bytes 17408 | tf_op jit(solution)/shard_map/all_gather | solution.py:114
  70.8 7.3 collective-permute-start.11
  92.2 5.3 collective-permute-start.14
  97.8 45.5 %gather_fusion.1 = f32[8192]{0:T(1024)S(1)} fusion(f32[8192]{0:T(1024)S(1)} %bitcast.133, s32[8192]{0:T(1024)S(1)} %broadcast_clamp_fusion), kind=kCustom, calls=%fused_computation.1 | custom fusion | bytes 98304 | tf_op jit(solution)/shard_map/gather | solution.py:98
  150.3 45.5 %gather_fusion.2 = f32[8192]{0:T(1024)S(1)} fusion(f32[16384]{0:T(1024)S(1)} %bitcast.135, s32[8192]{0:T(1024)S(1)} %broadcast_clamp_fusion.1), kind=kCustom, calls=%fused_computation.2 | custom fusion | bytes 98304 | tf_op jit(solution)/shard_map/gather | solution.py:109
  196.1 45.5 %gather_fusion = f32[8192]{0:T(1024)S(1)} fusion(f32[16384]{0:T(1024)S(1)} %bitcast.126, s32[8192]{0:T(1024)S(1)} %broadcast_clamp_fusion.1), kind=kCustom, calls=%fused_computation | custom fusion | bytes 98304 | tf_op jit(solution)/shard_map/gather | solution.py:96
  242.4 8.7 all-to-all-start
  252.8 8.0 all-to-all-done
  265.8 44.9 %scatter_custom_fusion.1 = f32[8192]{0:T(1024)S(1)} fusion(s32[8192]{0:T(1024)S(1)} %reshape.405, f32[8192]{0:T(1024)S(1)} %reshape.511, f32[]{:T(128)} %constant.152.clone.1), kind=kCustom, calls=%fused_computation.362 | custom fusion | flops 8192 | bytes 32772 | tf_op jit(solution)/shard_map/scatter-add | solution.py:103
  311.0 50.3 %scatter_fusion = f32[16384]{0:T(1024)S(1)} fusion(f32[16384]{0:T(1024)S(1)} %bitcast.127, s32[8192]{0:T(1024)S(1)} %reshape.501, f32[8192]{0:T(1024)S(1)} %reshape.503), kind=kCustom, calls=%fused_computation.13 | custom fusion | flops 8192 | bytes 131072 | tf_op jit(solution)/shard_map/scatter-add | solution.py:109
  369.0 9.8 collective-permute-start.20
  408.4 25.7 %all-gather.1 = f32[1,4096]{1,0:T(1,128)S(1)} all-gather(f32[1,256]{1,0:T(1,128)S(1)} %get-tuple-element.131), channel_id=3, replica_groups=mesh['row'=8,'col'=16] {'col'}, dimensions={1}, use_global_device_ids=true | all-gather | bytes 17408 | tf_op jit(solution)/shard_map/all_gather | solution.py:114
  436.0 5.2 collective-permute-start.31
  441.2 7.0 collective-permute-start.30
  448.2 45.5 %gather_fusion.6 = f32[8192]{0:T(1024)S(1)} fusion(f32[8192]{0:T(1024)S(1)} %bitcast.134, s32[8192]{0:T(1024)S(1)} %broadcast_clamp_fusion), kind=kCustom, calls=%fused_computation.6 | custom fusion | bytes 98304 | tf_op jit(solution)/shard_map/gather | solution.py:98
  506.6 45.5 %gather_fusion.3 = f32[8192]{0:T(1024)S(1)} fusion(f32[16384]{0:T(1024)S(1)} %bitcast.128, s32[8192]{0:T(1024)S(1)} %broadcast_clamp_fusion.1), kind=kCustom, calls=%fused_computation.3 | custom fusion | bytes 98304 | tf_op jit(solution)/shard_map/gather | solution.py:96
  552.9 10.8 %all-to-all-start.2 = ((f32[128,1,64]{2,1,0:T(1,128)}), f32[128,1,64]{2,1,0:T(1,128)S(1)}, u32[]{:S(2)}, u32[]{:S(2)}) async-start(f32[128,1,64]{2,1,0:T(1,128)} %bitcast.9), calls=%async_computation.2 | async-start | bytes 131072 | tf_op jit(solution)/shard_map/all_to_all | solution.py:99
  563.7 9.7 all-to-all-done.2
  578.5 44.9 %scatter_custom_fusion.3 = f32[8192]{0:T(1024)S(1)} fusion(s32[8192]{0:T(1024)S(1)} %reshape.405, f32[8192]{0:T(1024)S(1)} %reshape.527, f32[]{:T(128)} %constant.152.clone.1), kind=kCustom, calls=%fused_computation.360 | custom fusion | flops 8192 | bytes 32772 | tf_op jit(solution)/shard_map/scatter-add | solution.py:103
  623.6 50.3 %scatter_fusion.1 = f32[16384]{0:T(1024)S(1)} fusion(f32[16384]{0:T(1024)S(1)} %bitcast.129, s32[8192]{0:T(1024)S(1)} %reshape.501, f32[8192]{0:T(1024)S(1)} %reshape.519), kind=kCustom, calls=%fused_computation.15 | custom fusion | flops 8192 | bytes 131072 | tf_op jit(solution)/shard_map/scatter-add | solution.py:109
  681.6 9.8 collective-permute-start.36
  721.1 25.7 %all-gather.2 = f32[1,4096]{1,0:T(1,128)S(1)} all-gather(f32[1,256]{1,0:T(1,128)S(1)} %get-tuple-element.129), channel_id=4, replica_groups=mesh['row'=8,'col'=16] {'col'}, dimensions={1}, use_global_device_ids=true | all-gather | bytes 17408 | tf_op jit(solution)/shard_map/all_gather | solution.py:114
  753.9 7.0 collective-permute-start.46
  760.9 45.5 %gather_fusion.10 = f32[8192]{0:T(1024)S(1)} fusion(f32[8192]{0:T(1024)S(1)} %bitcast.132, s32[8192]{0:T(1024)S(1)} %broadcast_clamp_fusion), kind=kCustom, calls=%fused_computation.10 | custom fusion | bytes 98304 | tf_op jit(solution)/shard_map/gather | solution.py:98
  819.3 45.5 %gather_fusion.7 = f32[8192]{0:T(1024)S(1)} fusion(f32[16384]{0:T(1024)S(1)} %bitcast.130, s32[8192]{0:T(1024)S(1)} %broadcast_clamp_fusion.1), kind=kCustom, calls=%fused_computation.7 | custom fusion | bytes 98304 | tf_op jit(solution)/shard_map/gather | solution.py:96
  865.5 10.8 %all-to-all-start.5 = ((f32[128,1,64]{2,1,0:T(1,128)}), f32[128,1,64]{2,1,0:T(1,128)S(1)}, u32[]{:S(2)}, u32[]{:S(2)}) async-start(f32[128,1,64]{2,1,0:T(1,128)} %bitcast.28), calls=%async_computation.5 | async-start | bytes 131072 | tf_op jit(solution)/shard_map/all_to_all | solution.py:99
  876.4 9.7 all-to-all-done.5
  886.2 44.9 %scatter_custom_fusion.5 = f32[8192]{0:T(1024)S(1)} fusion(s32[8192]{0:T(1024)S(1)} %reshape.405, f32[8192]{0:T(1024)S(1)} %reshape.543, f32[]{:T(128)} %constant.152.clone.1), kind=kCustom, calls=%fused_computation.358 | custom fusion | flops 8192 | bytes 32772 | tf_op jit(solution)/shard_map/scatter-add | solution.py:103
  932.4 9.8 all-to-all-start.7
  943.0 8.9 all-to-all-done.7
  952.0 50.3 %scatter_fusion.2 = f32[16384]{0:T(1024)S(1)} fusion(f32[16384]{0:T(1024)S(1)} %bitcast.131, s32[8192]{0:T(1024)S(1)} %reshape.501, f32[8192]{0:T(1024)S(1)} %reshape.535), kind=kCustom, calls=%fused_computation.17 | custom fusion | flops 8192 | bytes 131072 | tf_op jit(solution)/shard_map/scatter-add | solution.py:109
  (281 shorter events, 186.7 us)
Async XLA Ops:
  1.4 24.6 %collective-permute-start.2 = (f32[1,256]{1,0:T(1,128)S(1)}, f32[1,256]{1,0:T(1,128)S(1)}, u32[]{:S(2)}, u32[]{:S(2)}) collective-permute-start(f32[1,256]{1,0:T(1,128)S(1)} %get-tuple-element.127), channel_id=1, source_target_pairs={{16,0},{32,16},{48,32},{64,48},{80,64},{96,80},{112,96},{17,1},{33... | collective-permute-start | bytes 3080 | tf_op jit(solution)/shard_map/ppermute | solution.py:31
  4.7 21.3 %collective-permute-start.1 = (f32[1,256]{1,0:T(1,128)S(1)}, f32[1,256]{1,0:T(1,128)S(1)}, u32[]{:S(2)}, u32[]{:S(2)}) collective-permute-start(f32[1,256]{1,0:T(1,128)S(1)} %get-tuple-element.126), channel_id=1, source_target_pairs={{0,16},{16,32},{32,48},{48,64},{64,80},{80,96},{96,112},{1,17},{17... | collective-permute-start | bytes 3080 | tf_op jit(solution)/shard_map/ppermute | solution.py:28
  8.5 23.2 %collective-permute-start = (f32[1,256]{1,0:T(1,128)S(1)}, f32[1,256]{1,0:T(1,128)S(1)}, u32[]{:S(2)}, u32[]{:S(2)}) collective-permute-start(f32[1,256]{1,0:T(1,128)S(1)} %slice.506), channel_id=1, source_target_pairs={{0,16},{16,32},{32,48},{48,64},{64,80},{80,96},{96,112},{1,17},{17... | collective-permute-start | bytes 3080 | tf_op jit(solution)/shard_map/ppermute | solution.py:20
  11.9 19.8 %collective-permute-start.3 = (f32[64,1]{1,0:T(8,128)S(1)}, f32[64,1]{1,0:T(8,128)S(1)}, u32[]{:S(2)}, u32[]{:S(2)}) collective-permute-start(f32[64,1]{1,0:T(8,128)S(1)} %slice.512), channel_id=1, source_target_pairs={{0,1},{1,2},{2,3},{3,4},{4,5},{5,6},{6,7},{7,8},{8,9},{9,10},{10,1... | collective-permute-start | bytes 776 | tf_op jit(solution)/shard_map/ppermute | solution.py:20
  15.8 226.5 %all-to-all-start.3 = ((f32[16,1,256]{2,1,0:T(1,128)}), f32[16,1,256]{2,1,0:T(1,128)S(1)}, u32[]{:S(2)}, u32[]{:S(2)}) async-start(f32[16,1,256]{2,1,0:T(1,128)} %stack.9), calls=%async_computation.3 | async-start | bytes 32768 | tf_op jit(solution)/shard_map/all_to_all | solution.py:14
  40.3 30.4 %collective-permute-start.9 = (f32[66,1]{1,0:T(8,128)S(1)}, f32[66,1]{1,0:T(8,128)S(1)}, u32[]{:S(2)}, u32[]{:S(2)}) collective-permute-start(f32[66,1]{1,0:T(8,128)S(1)} %get-tuple-element.101), channel_id=1, source_target_pairs={{1,0},{2,1},{3,2},{4,3},{5,4},{6,5},{7,6},{8,7},{9,8},{10,9},{11,1... | collective-permute-start | bytes 800 | tf_op jit(solution)/shard_map/ppermute | solution.py:31
  41.6 29.1 %collective-permute-start.8 = (f32[66,1]{1,0:T(8,128)S(1)}, f32[66,1]{1,0:T(8,128)S(1)}, u32[]{:S(2)}, u32[]{:S(2)}) collective-permute-start(f32[66,1]{1,0:T(8,128)S(1)} %get-tuple-element.100), channel_id=1, source_target_pairs={{0,1},{1,2},{2,3},{3,4},{4,5},{5,6},{6,7},{7,8},{8,9},{9,10},{10,1... | collective-permute-start | bytes 800 | tf_op jit(solution)/shard_map/ppermute | solution.py:28
  70.8 12.1 %collective-permute-start.11 = (f32[1,256]{1,0:T(1,128)S(1)}, f32[1,256]{1,0:T(1,128)S(1)}, u32[]{:S(2)}, u32[]{:S(2)}) collective-permute-start(f32[1,256]{1,0:T(1,128)S(1)} %get-tuple-element.123), channel_id=1, source_target_pairs={{16,0},{32,16},{48,32},{64,48},{80,64},{96,80},{112,96},{17,1},{33... | collective-permute-start | bytes 3080 | tf_op jit(solution)/shard_map/ppermute | solution.py:31
  90.3 54.0 %collective-permute-start.15 = (f32[1,256]{1,0:T(1,128)S(1)}, f32[1,256]{1,0:T(1,128)S(1)}, u32[]{:S(2)}, u32[]{:S(2)}) collective-permute-start(f32[1,256]{1,0:T(1,128)S(1)} %get-tuple-element.121), channel_id=1, source_target_pairs={{16,0},{32,16},{48,32},{64,48},{80,64},{96,80},{112,96},{17,1},{33... | collective-permute-start | bytes 3080 | tf_op jit(solution)/shard_map/ppermute | solution.py:31
  92.2 52.0 %collective-permute-start.14 = (f32[1,256]{1,0:T(1,128)S(1)}, f32[1,256]{1,0:T(1,128)S(1)}, u32[]{:S(2)}, u32[]{:S(2)}) collective-permute-start(f32[1,256]{1,0:T(1,128)S(1)} %get-tuple-element.120), channel_id=1, source_target_pairs={{0,16},{16,32},{32,48},{48,64},{64,80},{80,96},{96,112},{1,17},{17... | collective-permute-start | bytes 3080 | tf_op jit(solution)/shard_map/ppermute | solution.py:28
  144.4 51.5 %collective-permute-start.17 = (f32[66,1]{1,0:T(8,128)S(1)}, f32[66,1]{1,0:T(8,128)S(1)}, u32[]{:S(2)}, u32[]{:S(2)}) collective-permute-start(f32[66,1]{1,0:T(8,128)S(1)} %get-tuple-element.97), channel_id=1, source_target_pairs={{1,0},{2,1},{3,2},{4,3},{5,4},{6,5},{7,6},{8,7},{9,8},{10,9},{11,1... | collective-permute-start | bytes 800 | tf_op jit(solution)/shard_map/ppermute | solution.py:31
  145.7 50.3 %collective-permute-start.16 = (f32[66,1]{1,0:T(8,128)S(1)}, f32[66,1]{1,0:T(8,128)S(1)}, u32[]{:S(2)}, u32[]{:S(2)}) collective-permute-start(f32[66,1]{1,0:T(8,128)S(1)} %get-tuple-element.96), channel_id=1, source_target_pairs={{0,1},{1,2},{2,3},{3,4},{4,5},{5,6},{6,7},{7,8},{8,9},{9,10},{10,1... | collective-permute-start | bytes 800 | tf_op jit(solution)/shard_map/ppermute | solution.py:28
  242.4 18.4 %all-to-all-start = ((f32[128,1,64]{2,1,0:T(1,128)}), f32[128,1,64]{2,1,0:T(1,128)S(1)}, u32[]{:S(2)}, u32[]{:S(2)}) async-start(f32[128,1,64]{2,1,0:T(1,128)} %bitcast.2), calls=%async_computation | async-start | bytes 131072 | tf_op jit(solution)/shard_map/all_to_all | solution.py:99
  261.4 49.4 %all-to-all-start.1 = ((f32[128,1,64]{2,1,0:T(1,128)}), f32[128,1,64]{2,1,0:T(1,128)S(1)}, u32[]{:S(2)}, u32[]{:S(2)}) async-start(f32[128,1,64]{2,1,0:T(1,128)} %bitcast.5), calls=%async_computation.1 | async-start | bytes 131072 | tf_op jit(solution)/shard_map/all_to_all | solution.py:104
  367.7 11.3 %collective-permute-start.21 = (f32[66,1]{1,0:T(8,128)S(1)}, f32[66,1]{1,0:T(8,128)S(1)}, u32[]{:S(2)}, u32[]{:S(2)}) collective-permute-start(f32[66,1]{1,0:T(8,128)S(1)} %get-tuple-element.95), channel_id=1, source_target_pairs={{1,0},{2,1},{3,2},{4,3},{5,4},{6,5},{7,6},{8,7},{9,8},{10,9},{11,1... | collective-permute-start | bytes 800 | tf_op jit(solution)/shard_map/ppermute | solution.py:31
  369.0 10.9 %collective-permute-start.20 = (f32[66,1]{1,0:T(8,128)S(1)}, f32[66,1]{1,0:T(8,128)S(1)}, u32[]{:S(2)}, u32[]{:S(2)}) collective-permute-start(f32[66,1]{1,0:T(8,128)S(1)} %get-tuple-element.94), channel_id=1, source_target_pairs={{0,1},{1,2},{2,3},{3,4},{4,5},{5,6},{6,7},{7,8},{8,9},{9,10},{10,1... | collective-permute-start | bytes 800 | tf_op jit(solution)/shard_map/ppermute | solution.py:28
  402.6 33.3 %collective-permute-start.29 = (f32[66,1]{1,0:T(8,128)S(1)}, f32[66,1]{1,0:T(8,128)S(1)}, u32[]{:S(2)}, u32[]{:S(2)}) collective-permute-start(f32[66,1]{1,0:T(8,128)S(1)} %get-tuple-element.91), channel_id=1, source_target_pairs={{1,0},{2,1},{3,2},{4,3},{5,4},{6,5},{7,6},{8,7},{9,8},{10,9},{11,1... | collective-permute-start | bytes 800 | tf_op jit(solution)/shard_map/ppermute | solution.py:31
  403.8 32.0 %collective-permute-start.28 = (f32[66,1]{1,0:T(8,128)S(1)}, f32[66,1]{1,0:T(8,128)S(1)}, u32[]{:S(2)}, u32[]{:S(2)}) collective-permute-start(f32[66,1]{1,0:T(8,128)S(1)} %get-tuple-element.90), channel_id=1, source_target_pairs={{0,1},{1,2},{2,3},{3,4},{4,5},{5,6},{6,7},{7,8},{8,9},{9,10},{10,1... | collective-permute-start | bytes 800 | tf_op jit(solution)/shard_map/ppermute | solution.py:28
  436.0 62.2 %collective-permute-start.31 = (f32[1,256]{1,0:T(1,128)S(1)}, f32[1,256]{1,0:T(1,128)S(1)}, u32[]{:S(2)}, u32[]{:S(2)}) collective-permute-start(f32[1,256]{1,0:T(1,128)S(1)} %get-tuple-element.113), channel_id=1, source_target_pairs={{16,0},{32,16},{48,32},{64,48},{80,64},{96,80},{112,96},{17,1},{33... | collective-permute-start | bytes 3080 | tf_op jit(solution)/shard_map/ppermute | solution.py:31
  441.2 57.1 %collective-permute-start.30 = (f32[1,256]{1,0:T(1,128)S(1)}, f32[1,256]{1,0:T(1,128)S(1)}, u32[]{:S(2)}, u32[]{:S(2)}) collective-permute-start(f32[1,256]{1,0:T(1,128)S(1)} %get-tuple-element.112), channel_id=1, source_target_pairs={{0,16},{16,32},{32,48},{48,64},{64,80},{80,96},{96,112},{1,17},{17... | collective-permute-start | bytes 3080 | tf_op jit(solution)/shard_map/ppermute | solution.py:28
  494.5 10.2 %all-to-all-start.6 = ((f32[16,1,256]{2,1,0:T(1,128)}), f32[16,1,256]{2,1,0:T(1,128)S(1)}, u32[]{:S(2)}, u32[]{:S(2)}) async-start(f32[16,1,256]{2,1,0:T(1,128)} %stack.10), calls=%async_computation.6 | async-start | bytes 32768 | tf_op jit(solution)/shard_map/all_to_all | solution.py:14
  552.9 20.6 %all-to-all-start.2 = ((f32[128,1,64]{2,1,0:T(1,128)}), f32[128,1,64]{2,1,0:T(1,128)S(1)}, u32[]{:S(2)}, u32[]{:S(2)}) async-start(f32[128,1,64]{2,1,0:T(1,128)} %bitcast.9), calls=%async_computation.2 | async-start | bytes 131072 | tf_op jit(solution)/shard_map/all_to_all | solution.py:99
  574.1 49.4 %all-to-all-start.4 = ((f32[128,1,64]{2,1,0:T(1,128)}), f32[128,1,64]{2,1,0:T(1,128)S(1)}, u32[]{:S(2)}, u32[]{:S(2)}) async-start(f32[128,1,64]{2,1,0:T(1,128)} %bitcast.24), calls=%async_computation.4 | async-start | bytes 131072 | tf_op jit(solution)/shard_map/all_to_all | solution.py:104
  680.3 11.3 %collective-permute-start.37 = (f32[66,1]{1,0:T(8,128)S(1)}, f32[66,1]{1,0:T(8,128)S(1)}, u32[]{:S(2)}, u32[]{:S(2)}) collective-permute-start(f32[66,1]{1,0:T(8,128)S(1)} %get-tuple-element.87), channel_id=1, source_target_pairs={{1,0},{2,1},{3,2},{4,3},{5,4},{6,5},{7,6},{8,7},{9,8},{10,9},{11,1... | collective-permute-start | bytes 800 | tf_op jit(solution)/shard_map/ppermute | solution.py:31
  681.6 10.9 %collective-permute-start.36 = (f32[66,1]{1,0:T(8,128)S(1)}, f32[66,1]{1,0:T(8,128)S(1)}, u32[]{:S(2)}, u32[]{:S(2)}) collective-permute-start(f32[66,1]{1,0:T(8,128)S(1)} %get-tuple-element.86), channel_id=1, source_target_pairs={{0,1},{1,2},{2,3},{3,4},{4,5},{5,6},{6,7},{7,8},{8,9},{9,10},{10,1... | collective-permute-start | bytes 800 | tf_op jit(solution)/shard_map/ppermute | solution.py:28
  715.2 33.3 %collective-permute-start.45 = (f32[66,1]{1,0:T(8,128)S(1)}, f32[66,1]{1,0:T(8,128)S(1)}, u32[]{:S(2)}, u32[]{:S(2)}) collective-permute-start(f32[66,1]{1,0:T(8,128)S(1)} %get-tuple-element.83), channel_id=1, source_target_pairs={{1,0},{2,1},{3,2},{4,3},{5,4},{6,5},{7,6},{8,7},{9,8},{10,9},{11,1... | collective-permute-start | bytes 800 | tf_op jit(solution)/shard_map/ppermute | solution.py:31
  716.5 32.0 %collective-permute-start.44 = (f32[66,1]{1,0:T(8,128)S(1)}, f32[66,1]{1,0:T(8,128)S(1)}, u32[]{:S(2)}, u32[]{:S(2)}) collective-permute-start(f32[66,1]{1,0:T(8,128)S(1)} %get-tuple-element.82), channel_id=1, source_target_pairs={{0,1},{1,2},{2,3},{3,4},{4,5},{5,6},{6,7},{7,8},{8,9},{9,10},{10,1... | collective-permute-start | bytes 800 | tf_op jit(solution)/shard_map/ppermute | solution.py:28
  748.7 62.2 %collective-permute-start.47 = (f32[1,256]{1,0:T(1,128)S(1)}, f32[1,256]{1,0:T(1,128)S(1)}, u32[]{:S(2)}, u32[]{:S(2)}) collective-permute-start(f32[1,256]{1,0:T(1,128)S(1)} %get-tuple-element.105), channel_id=1, source_target_pairs={{16,0},{32,16},{48,32},{64,48},{80,64},{96,80},{112,96},{17,1},{33... | collective-permute-start | bytes 3080 | tf_op jit(solution)/shard_map/ppermute | solution.py:31
  753.9 57.1 %collective-permute-start.46 = (f32[1,256]{1,0:T(1,128)S(1)}, f32[1,256]{1,0:T(1,128)S(1)}, u32[]{:S(2)}, u32[]{:S(2)}) collective-permute-start(f32[1,256]{1,0:T(1,128)S(1)} %get-tuple-element.104), channel_id=1, source_target_pairs={{0,16},{16,32},{32,48},{48,64},{64,80},{80,96},{96,112},{1,17},{17... | collective-permute-start | bytes 3080 | tf_op jit(solution)/shard_map/ppermute | solution.py:28
  807.1 10.2 %all-to-all-start.8 = ((f32[16,1,256]{2,1,0:T(1,128)}), f32[16,1,256]{2,1,0:T(1,128)S(1)}, u32[]{:S(2)}, u32[]{:S(2)}) async-start(f32[16,1,256]{2,1,0:T(1,128)} %stack.11), calls=%async_computation.8 | async-start | bytes 32768 | tf_op jit(solution)/shard_map/all_to_all | solution.py:14
  865.5 20.6 %all-to-all-start.5 = ((f32[128,1,64]{2,1,0:T(1,128)}), f32[128,1,64]{2,1,0:T(1,128)S(1)}, u32[]{:S(2)}, u32[]{:S(2)}) async-start(f32[128,1,64]{2,1,0:T(1,128)} %bitcast.28), calls=%async_computation.5 | async-start | bytes 131072 | tf_op jit(solution)/shard_map/all_to_all | solution.py:99
  932.4 19.5 %all-to-all-start.7 = ((f32[128,1,64]{2,1,0:T(1,128)}), f32[128,1,64]{2,1,0:T(1,128)S(1)}, u32[]{:S(2)}, u32[]{:S(2)}) async-start(f32[128,1,64]{2,1,0:T(1,128)} %bitcast.37), calls=%async_computation.7 | async-start | bytes 131072 | tf_op jit(solution)/shard_map/all_to_all | solution.py:104
  (40 other events, 267.3 us)
